TPU v7x, 32 devices: a whole 2x2x4 slice. The times are simulated.
32 devices in a mesh: pb: 4 (over y, core), ctx: 8 (over z, x).
Axes of the slice: x: 2, y: 2, z: 4, core: 2. Of those that a mesh axis runs over, the one named last changes fastest.
Arguments:
- queries: bfloat16 [32768, 1024], P(('pb', 'ctx')), may hold values from -64 to 64
- key_states: bfloat16 [32768, 128], P(('pb', 'ctx')), may hold values from -6 to 6
- value_states: bfloat16 [32768, 128], P(('pb', 'ctx')), may hold values from -6 to 6
- key_blocks: int32 [256, 8], replicated, may hold values from -1 to 255, as said below
Outputs:
- attended: bfloat16 [32768, 1024], P(('pb', 'ctx'))
Inputs may be any that keep to these rules, and one draw needn't show every extreme that they name: `key_blocks`: row i lists first the blocks 0 to 1, then those of blocks i - 1, i, i + 1 that exist and are not among them, in increasing order, then 3 distinct blocks of other devices with the same pb index, none among those already listed and none next to the device's own 8 blocks; -1 fills the rest. Over the 8 rows of one device, at most 4 of the random entries name blocks of any one other device, and every device reaches that.
All inputs are finite; a program needn't handle non-finite values.
Results may differ from a plain program's by a relative error of at most 0.0047.
Values may be sent and summed in bfloat16 or wider, within the bound.
No kernel may reach another device: no remote copies, remote signals or barrier semaphores. Data moves between devices by JAX's collectives and lax.ppermute only.
A program may use at most 128 MiB of HBM per device.

v0:
```python
import jax
import jax.numpy as jnp
from jax import lax
from jax.sharding import PartitionSpec as P

HEAD_DIM = 128
HEADS = 8
BLOCK = 128
GLOBAL = 2
RANDOM = 3
LIST = 8


def extended(shard, sides, width):
    for axis, dim in sides:
        devices, length = (lax.axis_size(axis), shard.shape[dim])
        up = [(i, (i + 1) % devices) for i in range(devices - 1)]
        down = [(j, i) for i, j in up]
        last = lax.slice_in_dim(shard, length - width, length, axis=dim)
        first = lax.slice_in_dim(shard, 0, width, axis=dim)
        before = lax.ppermute(last, axis, up)
        after = lax.ppermute(first, axis, down)
        shard = jnp.concatenate([before, shard, after], axis=dim)
    return shard


def spread(shard, axis, root):
    mine = lax.axis_index(axis) == root
    return lax.psum(jnp.where(mine, shard, jnp.zeros_like(shard)), axis)


def attend(query_block, key_rows, value_rows, key_mask):
    scores = jnp.einsum(
        "thd,ud->thu", query_block, key_rows, preferred_element_type=jnp.float32
    ) * HEAD_DIM ** (-0.5)
    scores = jnp.where(key_mask[None, None, :], scores, -1e30)
    row_max = jnp.max(scores, axis=-1, keepdims=True)
    weights = jnp.exp(scores - row_max)
    normalizer = jnp.sum(weights, axis=-1, keepdims=True)
    rounded = weights.astype(jnp.bfloat16)
    result = (
        jnp.einsum("thu,ud->thd", rounded, value_rows, preferred_element_type=jnp.float32)
        / normalizer
    )
    return result.astype(jnp.bfloat16)


def classify(entries, first_block, blocks_dev, ctx_count):
    usable = entries >= 0
    is_global = usable & (entries < GLOBAL)
    nearby = usable & (entries >= first_block - 1) & (entries <= first_block + blocks_dev)
    remote = usable & jnp.logical_not(is_global) & jnp.logical_not(nearby)
    holder = jnp.maximum(entries, 0) // blocks_dev % ctx_count
    owner_hits = ((holder[:, None] == jnp.arange(ctx_count)[None, :]) & remote[:, None]).astype(
        jnp.int32
    )
    slot_rank = jnp.sum(jnp.cumsum(owner_hits, axis=0) * owner_hits, axis=1) - 1
    return (usable, is_global, nearby, remote, holder, slot_rank)


def per_device(queries, key_states, value_states, key_blocks):
    blocks_dev = queries.shape[0] // BLOCK
    ctx_count = lax.axis_size("ctx")
    slot_most = (RANDOM * blocks_dev + ctx_count - 2) // (ctx_count - 1)
    device_now = lax.axis_index(("pb", "ctx"))
    column_now = lax.axis_index("ctx")
    own_first = device_now * blocks_dev
    group_first = (device_now - column_now) * blocks_dev
    local_kv = jnp.stack(
        [
            key_states.reshape(blocks_dev, BLOCK, HEAD_DIM),
            value_states.reshape(blocks_dev, BLOCK, HEAD_DIM),
        ]
    )
    padded = extended(local_kv, ((("pb", "ctx"), 1),), 1)
    shared = spread(local_kv[:, :GLOBAL], ("pb", "ctx"), 0)
    own_rows = lax.dynamic_slice_in_dim(key_blocks, own_first, blocks_dev, 0)
    own_list = own_rows.reshape(-1)
    usable, is_global, nearby, remote, holder, slot_rank = classify(
        own_list, own_first, blocks_dev, ctx_count
    )
    slot_ids = jnp.arange(slot_most)
    matched = (
        remote[:, None, None]
        & (holder[:, None, None] == jnp.arange(ctx_count)[None, :, None])
        & (slot_rank[:, None, None] == slot_ids[None, None, :])
    )
    group_index = jnp.sum(
        matched.astype(jnp.int32) * (own_list - group_first)[:, None, None], axis=0
    ).reshape(-1)
    filled = jnp.any(matched, axis=0).reshape(-1)
    empty_pool = jnp.zeros((2, ctx_count * slot_most, BLOCK, HEAD_DIM), jnp.bfloat16)
    shard_piece = lax.all_gather(local_kv, "ctx", axis=1, tiled=True)
    piece_len = shard_piece.shape[1]
    inside = filled & (group_index >= 0) & (group_index < piece_len)
    taken_blocks = jnp.take(shard_piece, jnp.clip(group_index, 0, piece_len - 1), axis=1)
    window_new = jnp.where(inside[None, :, None, None], taken_blocks, empty_pool)
    kv_pool = jnp.concatenate([padded, shared, window_new], axis=1)
    pool_size = kv_pool.shape[1]
    global_index = blocks_dev + 2 + own_list
    near_index = own_list - (own_first - 1)
    remote_index = blocks_dev + 2 + GLOBAL + holder * slot_most + slot_rank
    pool_index = jnp.where(is_global, global_index, jnp.where(nearby, near_index, remote_index))
    pool_index = jnp.clip(jnp.where(usable, pool_index, 0), 0, pool_size - 1).reshape(
        blocks_dev, LIST
    )
    usable_rows = usable.reshape(blocks_dev, LIST)
    query_cube = queries.reshape(blocks_dev, BLOCK, HEADS, HEAD_DIM)

    def per_block(inputs):
        query_block, row_index, row_usable = inputs
        selected = jnp.take(kv_pool, row_index, axis=1)
        key_rows = selected[0].reshape(LIST * BLOCK, HEAD_DIM)
        value_rows = selected[1].reshape(LIST * BLOCK, HEAD_DIM)
        key_mask = jnp.repeat(row_usable, BLOCK)
        return attend(query_block, key_rows, value_rows, key_mask)

    result = lax.map(per_block, (query_cube, pool_index, usable_rows))
    return result.reshape(blocks_dev * BLOCK, HEADS * HEAD_DIM)


def solution(mesh):
    in_specs = (P(("pb", "ctx"), None), P(("pb", "ctx"), None), P(("pb", "ctx"), None), P())
    out_specs = P(("pb", "ctx"), None)
    return jax.shard_map(
        per_device, mesh=mesh, in_specs=in_specs, out_specs=out_specs, check_vma=False
    )
```

profile of v0, /device:TPU:0, one launch (start us, length us, event | category | flops | bytes accessed | tf_op | source)
XLA Modules:
  0.0 246.7 jit_solution(3679912432769475257)
XLA Ops:
  7.4 1.0 fusion.22
  8.3 4.8 %collective-permute-start = (bf16[2,1,128,128]{3,2,0,1:T(8,128)(2,1)S(1)}, bf16[2,1,128,128]{3,2,0,1:T(8,128)(2,1)S(1)}, u32[]{:S(2)}, u32[]{:S(2)}) collective-permute-start(bf16[2,1,128,128]{3,2,0,1:T(8,128)(2,1)S(1)} %get-tuple-element.75), channel_id=1, source_target_pairs={{0,1},{1,2},{2,3},{3,4},{4,5},{5,6},{6,7},{7,8},{8,9},{9,10},{10,1... | collective-permute-start | bytes 196616 | tf_op jit(solution)/shard_map/ppermute | solution.py:21
  13.2 1.5 fusion.20
  15.7 2.4 pad_maximum_fusion
  18.1 1.3 collective-permute-start.1
  21.6 1.9 copy.30
  23.6 1.1 collective-permute-done.1
  25.3 150.8 %all-reduce.2.cloned.1.call-done = bf16[2,2,128,128]{3,2,0,1:T(8,128)(2,1)} async-done(((bf16[2,2,128,128]{3,2,0,1:T(8,128)(2,1)}), bf16[2,2,128,128]{3,2,0,1:T(8,128)(2,1)}) %all-reduce.2.cloned.1.call-update) | async-done | bytes 131088 | tf_op jit(solution)/shard_map/psum | solution.py:29
  176.1 1.6 constant_dynamic-update-slice_fusion
  177.7 4.7 %copy.22 = bf16[2,64,128,128]{3,2,1,0:T(8,128)(2,1)} copy(bf16[2,64,128,128]{3,2,0,1:T(8,128)(2,1)} %all-gather.2.cloned.1.call-done) | data formatting | bytes 8388608 | tf_op jit(solution)/shard_map/all_gather | solution.py:93
  182.4 3.1 %gather_fusion.1 = bf16[32,2,128,128]{3,2,1,0:T(8,128)(2,1)S(1)} fusion(bf16[2,64,128,128]{3,2,1,0:T(8,128)(2,1)} %copy.22, s32[1024]{0:T(1024)S(1)} %pad_clamp_fusion.1), kind=kCustom, calls=%fused_computation.1 | custom fusion | bytes 4194432 | tf_op jit(solution)/shard_map/jit(_take)/gather | solution.py:96
  185.6 2.4 bitcast_dynamic-update-slice_fusion
  188.0 2.0 copy.24
  190.0 45.7 %while.10 = (s32[]{:T(128)}, bf16[8,128,8,128]{3,2,1,0:T(8,128)(2,1)}, pred[8,8]{1,0:T(8,128)(4,1)S(1)}, bf16[8,128,8,128]{3,2,1,0:T(8,128)(2,1)}, s32[8,8]{1,0:...) while((s32[]{:T(128)}, bf16[8,128,8,128]{3,2,1,0:T(8,128)(2,1)}, pred[8,8]{1,0:T(8,128)(4,1)S(1)}, ...), condition=%wide.region_8.9_spmd, body=%wide.region_5.8_spmd.sunk | while | flops 548928576 | bytes 17855268 | solution.py:118
  190.9 1.0 constant_dynamic-slice_fusion.4
  192.8 1.1 fusion.54
  193.8 1.0 fusion.55
  198.5 1.1 fusion.54
  199.5 1.0 fusion.55
  204.2 1.1 fusion.54
  205.2 1.0 fusion.55
  209.9 1.1 fusion.54
  210.9 1.0 fusion.55
  215.6 1.1 fusion.54
  216.6 1.0 fusion.55
  221.3 1.1 fusion.54
  222.4 1.0 fusion.55
  227.0 1.1 fusion.54
  228.1 1.0 fusion.55
  232.7 1.1 fusion.54
  233.8 1.0 fusion.55
  235.7 3.5 %copy.38 = bf16[128,8,8,128]{3,1,2,0:T(8,128)(2,1)} copy(bf16[128,8,8,128]{3,2,1,0:T(8,128)(2,1)} %bitcast.22) | data formatting | bytes 4194304
  (133 shorter events, 31.6 us)
Async XLA Ops:
  7.4 12.1 %copy-start = (s32[256,8]{0,1:T(8,128)S(1)}, s32[256,8]{0,1:T(8,128)}, u32[]{:S(2)}) copy-start(s32[256,8]{0,1:T(8,128)} %param.9) | copy-start | bytes 24580
  7.4 14.2 %copy-start.1 = (bf16[1024,1024]{1,0:T(8,128)(2,1)S(1)}, bf16[1024,1024]{1,0:T(8,128)(2,1)}, u32[]{:S(2)}) copy-start(bf16[1024,1024]{1,0:T(8,128)(2,1)} %param.6) | copy-start | bytes 6291460
  7.4 168.7 %all-reduce.2.cloned.1.call-start = ((), (), s32[]{:S(2)}) async-start(), calls=%async_computation | async-start | bytes 262144 | tf_op jit(solution)/shard_map/psum | solution.py:29
  8.3 6.7 %collective-permute-start = (bf16[2,1,128,128]{3,2,0,1:T(8,128)(2,1)S(1)}, bf16[2,1,128,128]{3,2,0,1:T(8,128)(2,1)S(1)}, u32[]{:S(2)}, u32[]{:S(2)}) collective-permute-start(bf16[2,1,128,128]{3,2,0,1:T(8,128)(2,1)S(1)} %get-tuple-element.75), channel_id=1, source_target_pairs={{0,1},{1,2},{2,3},{3,4},{4,5},{5,6},{6,7},{7,8},{8,9},{9,10},{10,1... | collective-permute-start | bytes 196616 | tf_op jit(solution)/shard_map/ppermute | solution.py:21
  14.8 162.9 %all-gather.2.cloned.1.call-start = ((), (), s32[]{:S(2)}) async-start(), calls=%async_computation.1 | async-start | bytes 4718592 | tf_op jit(solution)/shard_map/all_gather | solution.py:93
  18.1 6.6 %collective-permute-start.1 = (bf16[2,1,128,128]{3,2,0,1:T(8,128)(2,1)S(1)}, bf16[2,1,128,128]{3,2,0,1:T(8,128)(2,1)S(1)}, u32[]{:S(2)}, u32[]{:S(2)}) collective-permute-start(bf16[2,1,128,128]{3,2,0,1:T(8,128)(2,1)S(1)} %get-tuple-element.74), channel_id=1, source_target_pairs={{1,0},{2,1},{3,2},{4,3},{5,4},{6,5},{7,6},{8,7},{9,8},{10,9},{11,1... | collective-permute-start | bytes 196616 | tf_op jit(solution)/shard_map/ppermute | solution.py:22
Sparse Core Ops, SparseCore 0:
  14.9 161.1 all-reduce.1
Sparse Core Ops, SparseCore 1:
  18.2 75.2 all-gather.1
where the time goes:
time: 247 us
  waiting for transfers between devices  152 us (62%)
  local copies, waits for them, and re-layouts  40.5 us (16%)
  other arithmetic  17.7 us (7%)
  between operations  15 us (6%)
  matrix products  14.8 us (6%)
  starting transfers between devices  6.18 us (3%)
    psum x1, waiting for transfers between devices, spread(): return lax.psum(jnp.where(mine, shard, jnp.zeros_like(shard)), axis)  151 us
    reduce_sum x8, other arithmetic, attend(): normalizer = jnp.sum(weights, axis=-1, keepdims=True)  8.41 us
    unnamed x10, local copies, waits for them, and re-layouts  8.39 us
    dot_general x8, matrix products, attend(): jnp.einsum('thu,ud->thd', rounded, value_rows, preferred_element_type=jnp...  8.04 us
    dynamic_slice x8, local copies, waits for them, and re-layouts, per_device(): result = lax.map(per_block, (query_cube, pool_index, usable_rows))  7.74 us
    dynamic_update_slice x8, local copies, waits for them, and re-layouts, per_device(): result = lax.map(per_block, (query_cube, pool_index, usable_rows))  7.07 us
    dot_general x8, matrix products, attend(): jnp.einsum('thd,ud->thu', query_block, key_rows, preferred_element_type=j...  6.75 us
    gather x8, local copies, waits for them, and re-layouts, per_block(): selected = jnp.take(kv_pool, row_index, axis=1)  5.18 us
  transfers between devices with their start and end apart: 4, of which 3 were waited for; matrix products, arithmetic and copies ran while one was open for 4% of the time, Pallas kernels for 0%

commit v1 on v0

--- a/solution.py
+++ b/solution.py
@@ -26,7 +26,7 @@
 
 def spread(shard, axis, root):
     mine = lax.axis_index(axis) == root
-    return lax.psum(jnp.where(mine, shard, jnp.zeros_like(shard)), axis)
+    return jnp.sum(lax.all_gather(jnp.where(mine, shard, jnp.zeros_like(shard)), axis), axis=0)
 
 
 def attend(query_block, key_rows, value_rows, key_mask):

time: 247 us -> 221 us (0.89)
  waiting for transfers between devices: 152 us -> 126 us
    psum x1 -> x0, waiting for transfers between devices: 151 us -> none  [spread(): return lax.psum(jnp.where(mine, shard, jnp.zeros_like(shard)), axis)]
    all_gather x1, waiting for transfers between devices: 0.01 us -> 67.8 us  [per_device(): shard_piece = lax.all_gather(local_kv, 'ctx', axis=1, tiled=True)]
    all_gather x0 -> x1, waiting for transfers between devices: none -> 55.4 us  [spread(): lax.all_gather(jnp.where(mine, shard, jnp.zeros_like(shard)), axis)]
    reduce_sum x0 -> x1, other arithmetic: none -> 2.89 us  [spread(): jnp.sum(lax.all_gather(jnp.where(mine, shard, jnp.zeros_like(shard)), axi...]
    unnamed x10 -> x14, local copies, waits for them, and re-layouts: 8.39 us -> 7.48 us
  transfers between devices with their start and end apart: 4 -> 4, of which waited for: 3 -> 4; matrix products, arithmetic and copies ran while one was open for 4% -> 6% of each run, Pallas kernels for 0% -> 0%
where the time goes in v1:
time: 221 us; the launch traced here: 220 us
  waiting for transfers between devices  126 us (57%)
  local copies, waits for them, and re-layouts  39.6 us (18%)
  other arithmetic  19.6 us (9%)
  matrix products  14.8 us (7%)
  between operations  13.6 us (6%)
  starting transfers between devices  6.21 us (3%)
    all_gather x1, waiting for transfers between devices, per_device(): shard_piece = lax.all_gather(local_kv, 'ctx', axis=1, tiled=True)  67.8 us
    all_gather x1, waiting for transfers between devices, spread(): lax.all_gather(jnp.where(mine, shard, jnp.zeros_like(shard)), axis)  55.4 us
    reduce_sum x8, other arithmetic, attend(): normalizer = jnp.sum(weights, axis=-1, keepdims=True)  8.41 us
    dot_general x8, matrix products, attend(): jnp.einsum('thu,ud->thd', rounded, value_rows, preferred_element_type=jnp...  8.03 us
    dynamic_slice x8, local copies, waits for them, and re-layouts, per_device(): result = lax.map(per_block, (query_cube, pool_index, usable_rows))  7.74 us
    unnamed x14, local copies, waits for them, and re-layouts  7.48 us
    dynamic_update_slice x8, local copies, waits for them, and re-layouts, per_device(): result = lax.map(per_block, (query_cube, pool_index, usable_rows))  7.06 us
    dot_general x8, matrix products, attend(): jnp.einsum('thd,ud->thu', query_block, key_rows, preferred_element_type=j...  6.75 us
  transfers between devices with their start and end apart: 4, of which 4 were waited for; matrix products, arithmetic and copies ran while one was open for 6% of the time, Pallas kernels for 0%

profile of v1, /device:TPU:0, one launch (start us, length us, event | category | flops | bytes accessed | tf_op | source)
XLA Modules:
  0.0 220.2 jit_solution(2560867852864975366)
XLA Ops:
  6.6 1.0 fusion.22
  7.6 4.8 %collective-permute-start = (bf16[2,1,128,128]{3,2,0,1:T(8,128)(2,1)S(1)}, bf16[2,1,128,128]{3,2,0,1:T(8,128)(2,1)S(1)}, u32[]{:S(2)}, u32[]{:S(2)}) collective-permute-start(bf16[2,1,128,128]{3,2,0,1:T(8,128)(2,1)S(1)} %get-tuple-element.75), channel_id=1, source_target_pairs={{0,1},{1,2},{2,3},{3,4},{4,5},{5,6},{6,7},{7,8},{8,9},{9,10},{10,1... | collective-permute-start | bytes 196616 | tf_op jit(solution)/shard_map/ppermute | solution.py:21
  12.4 1.9 collective-permute-done
  14.9 2.3 %pad_maximum_fusion = (bf16[2,8,128,128]{3,2,0,1:T(8,128)(2,1)}, bf16[2,44,128,128]{3,2,0,1:T(8,128)(2,1)}) fusion(bf16[1,8,128,128]{3,2,0,1:T(8,128)(2,1)} %bitcast.71, bf16[1,8,128,128]{3,2,0,1:T(8,128)(2,1)} %bitcast.74, bf16[2,44,128,128]{3,2,0,1:T(8,128)(2,1)} %constant_dynamic-update-slice_fusion.3), kind=kLoop, calls=%fused_computation.32 | loop fusion | flops 1048576 | bytes 1572864 | tf_op jit(solution)/shard_map/stack | solution.py:69
  18.0 1.3 collective-permute-start.1
  21.5 1.9 copy.31
  23.5 1.0 collective-permute-done.1
  25.2 67.8 %all-gather.4.cloned.1.call-done = bf16[2,64,128,128]{3,2,0,1:T(8,128)(2,1)} async-done(((bf16[2,8,128,128]{3,2,0,1:T(8,128)(2,1)}), bf16[2,64,128,128]{3,2,0,1:T(8,128)(2,1)}) %all-gather.4.cloned.1.call-update) | async-done | bytes 4194320 | tf_op jit(solution)/shard_map/all_gather | solution.py:93
  92.9 4.7 %copy.22 = bf16[2,64,128,128]{3,2,1,0:T(8,128)(2,1)} copy(bf16[2,64,128,128]{3,2,0,1:T(8,128)(2,1)} %all-gather.4.cloned.1.call-done) | data formatting | bytes 8388608 | tf_op jit(solution)/shard_map/all_gather | solution.py:93
  97.7 3.1 %gather_fusion.1 = bf16[32,2,128,128]{3,2,1,0:T(8,128)(2,1)S(1)} fusion(bf16[2,64,128,128]{3,2,1,0:T(8,128)(2,1)} %copy.22, s32[1024]{0:T(1024)S(1)} %pad_clamp_fusion.1), kind=kCustom, calls=%fused_computation.1 | custom fusion | bytes 4194432 | tf_op jit(solution)/shard_map/jit(_take)/gather | solution.py:96
  100.8 55.4 %all-gather.6.cloned.1.call-done = bf16[64,2,128,128]{3,2,0,1:T(8,128)(2,1)} async-done(((bf16[2,2,128,128]{3,2,0,1:T(8,128)(2,1)}), bf16[64,2,128,128]{3,2,0,1:T(8,128)(2,1)}) %all-gather.6.cloned.1.call-update) | async-done | bytes 4194320 | tf_op jit(solution)/shard_map/all_gather | solution.py:29
  156.2 2.9 %reduce_sum.40 = bf16[2,2,128,128]{3,2,0,1:T(8,128)(2,1)S(1)} reduce(bf16[32,2,2,128,128]{4,3,1,0,2:T(8,128)(2,1)} %bitcast.69, bf16[]{:T(256)} %constant.114.clone.1), dimensions={0}, to_apply=%region_2.3 | reduce | flops 2031616 | bytes 4325378 | tf_op jit(solution)/shard_map/reduce_sum | solution.py:29
  159.8 2.4 %bitcast_dynamic-update-slice_fusion = bf16[2,44,128,128]{3,2,0,1:T(8,128)(2,1)} fusion(bf16[2,44,128,128]{3,2,0,1:T(8,128)(2,1)} %constant_dynamic-update-slice_fusion, bf16[32,2,128,128]{3,2,1,0:T(8,128)(2,1)S(1)} %gather_fusion.1, pred[32]{0:T(512)(128)(4,1)S(1)} %and.198, pred[32]{0:T(512)(128)(4,1)S(1)} %compare_and_fusion.1), kind=kLoop, calls=%fused_computation.28 | loop fusion | flops 2097152 | bytes 4194368 | tf_op jit(solution)/shard_map/concatenate | solution.py:98
  162.1 2.0 copy.24
  164.1 45.7 %while.10 = (s32[]{:T(128)}, bf16[8,128,8,128]{3,2,1,0:T(8,128)(2,1)}, pred[8,8]{1,0:T(8,128)(4,1)S(1)}, bf16[8,128,8,128]{3,2,1,0:T(8,128)(2,1)}, s32[8,8]{1,0:...) while((s32[]{:T(128)}, bf16[8,128,8,128]{3,2,1,0:T(8,128)(2,1)}, pred[8,8]{1,0:T(8,128)(4,1)S(1)}, ...), condition=%wide.region_8.9_spmd, body=%wide.region_5.8_spmd.sunk | while | flops 548928576 | bytes 17855268 | solution.py:118
  166.9 1.1 fusion.54
  168.0 1.0 fusion.55
  172.6 1.1 fusion.54
  173.7 1.0 fusion.55
  178.4 1.1 fusion.54
  179.4 1.0 fusion.55
  184.1 1.1 fusion.54
  185.1 1.0 fusion.55
  189.8 1.1 fusion.54
  190.8 1.0 fusion.55
  195.5 1.1 fusion.54
  196.6 1.0 fusion.55
  201.2 1.1 fusion.54
  202.3 1.0 fusion.55
  206.9 1.1 fusion.54
  208.0 1.0 fusion.55
  209.9 3.5 %copy.39 = bf16[128,8,8,128]{3,1,2,0:T(8,128)(2,1)} copy(bf16[128,8,8,128]{3,2,1,0:T(8,128)(2,1)} %bitcast.23) | data formatting | bytes 4194304
  (138 shorter events, 33.7 us)
Async XLA Ops:
  6.5 12.8 %copy-start = (s32[256,8]{0,1:T(8,128)S(1)}, s32[256,8]{0,1:T(8,128)}, u32[]{:S(2)}) copy-start(s32[256,8]{0,1:T(8,128)} %param.9) | copy-start | bytes 24580
  6.5 10.8 %copy-start.2 = (bf16[1024,128]{1,0:T(8,128)(2,1)S(1)}, bf16[1024,128]{1,0:T(8,128)(2,1)}, u32[]{:S(2)}) copy-start(bf16[1024,128]{1,0:T(8,128)(2,1)} %param.7) | copy-start | bytes 786436
  6.5 10.8 %copy-start.1 = (bf16[1024,128]{1,0:T(8,128)(2,1)S(1)}, bf16[1024,128]{1,0:T(8,128)(2,1)}, u32[]{:S(2)}) copy-start(bf16[1024,128]{1,0:T(8,128)(2,1)} %param.8) | copy-start | bytes 786436
  6.5 15.0 %copy-start.3 = (bf16[1024,1024]{1,0:T(8,128)(2,1)S(1)}, bf16[1024,1024]{1,0:T(8,128)(2,1)}, u32[]{:S(2)}) copy-start(bf16[1024,1024]{1,0:T(8,128)(2,1)} %param.6) | copy-start | bytes 6291460
  6.5 86.4 %all-gather.4.cloned.1.call-start = ((), (), s32[]{:S(2)}) async-start(), calls=%async_computation | async-start | bytes 4718592 | tf_op jit(solution)/shard_map/all_gather | solution.py:93
  7.6 6.7 %collective-permute-start = (bf16[2,1,128,128]{3,2,0,1:T(8,128)(2,1)S(1)}, bf16[2,1,128,128]{3,2,0,1:T(8,128)(2,1)S(1)}, u32[]{:S(2)}, u32[]{:S(2)}) collective-permute-start(bf16[2,1,128,128]{3,2,0,1:T(8,128)(2,1)S(1)} %get-tuple-element.75), channel_id=1, source_target_pairs={{0,1},{1,2},{2,3},{3,4},{4,5},{5,6},{6,7},{7,8},{8,9},{9,10},{10,1... | collective-permute-start | bytes 196616 | tf_op jit(solution)/shard_map/ppermute | solution.py:21
  17.3 138.9 %all-gather.6.cloned.1.call-start = ((), (), s32[]{:S(2)}) async-start(), calls=%async_computation.1 | async-start | bytes 4325376 | tf_op jit(solution)/shard_map/all_gather | solution.py:29
  18.0 6.5 %collective-permute-start.1 = (bf16[2,1,128,128]{3,2,0,1:T(8,128)(2,1)S(1)}, bf16[2,1,128,128]{3,2,0,1:T(8,128)(2,1)S(1)}, u32[]{:S(2)}, u32[]{:S(2)}) collective-permute-start(bf16[2,1,128,128]{3,2,0,1:T(8,128)(2,1)S(1)} %get-tuple-element.74), channel_id=1, source_target_pairs={{1,0},{2,1},{3,2},{4,3},{5,4},{6,5},{7,6},{8,7},{9,8},{10,9},{11,1... | collective-permute-start | bytes 196616 | tf_op jit(solution)/shard_map/ppermute | solution.py:22
Sparse Core Ops, SparseCore 0:
  17.4 75.5 all-gather.3
  96.0 60.1 all-gather.5
